TPU v7x, 128 devices: a whole 4x4x4 slice. The times are simulated.
128 devices in a mesh: gx: 2 (over core), gy: 16 (over y, x), gz: 4 (over z).
Axes of the slice: x: 4, y: 4, z: 4, core: 2. Of those that a mesh axis runs over, the one named last changes fastest.
Arguments:
- places: float32 [3, 12, 16, 24, 128], P(None, 'gx', 'gy', 'gz'), may hold values from 0.45 to 8.35, as said below
- velocity: float32 [3, 12, 16, 24, 128], P(None, 'gx', 'gy', 'gz'), may hold values from -6 to 6
- forces_old: float32 [3, 12, 16, 24, 128], P(None, 'gx', 'gy', 'gz'), may hold values from -48 to 48
- counts: int32 [12, 16, 24], P('gx', 'gy', 'gz'), may hold values from 16 to 120, as said below
- mig_atom: int32 [2, 16, 4, 16], P('gx', 'gy', 'gz'), may hold values from 0 to 4607, as said below
- mig_face: int32 [2, 16, 4, 16], P('gx', 'gy', 'gz'), may hold values from 0 to 5, as said below
Outputs:
- new_places: float32 [3, 12, 16, 24, 128], P(None, 'gx', 'gy', 'gz')
- new_velocity: float32 [3, 12, 16, 24, 128], P(None, 'gx', 'gy', 'gz')
- new_forces: float32 [3, 12, 16, 24, 128], P(None, 'gx', 'gy', 'gz')
Inputs may be any that keep to these rules, and one draw needn't show every extreme that they name: `places`: within a cell and between neighbouring cells, any two slots lie at least 0.7 apart. `counts`: some cell holds exactly 120 atoms. `mig_atom`: each device's 16 entries name occupied slots of 16 distinct cells. `mig_face`: each entry's cell lies on the named face of its device's block.
All inputs are finite; a program needn't handle non-finite values.
Results may differ from a plain program's by a relative error of at most 0.0003.
Values sent between devices are 32-bit elements; how exact they have to be, the bound alone decides.
A program may use at most 64 MiB of HBM per device.

v0:
```python
import math

import jax
import jax.numpy as jnp
from jax import lax
from jax.sharding import PartitionSpec as P

step_size = 0.005
cut_radius = 2.5
spacing = 1.1
edge_force = 24.0 * (2.0 * cut_radius ** (-13) - cut_radius ** (-7))


def with_halo(value, sides, width):
    edges = {}
    for axis, dim in sides:
        devices, length = (lax.axis_size(axis), value.shape[dim])
        up = [(i, (i + 1) % devices) for i in range(devices)]
        last = lax.slice_in_dim(value, length - width, length, axis=dim)
        initial = lax.slice_in_dim(value, 0, width, axis=dim)
        edges[dim] = (
            lax.ppermute(last, axis, up),
            lax.ppermute(initial, axis, [(b, a) for a, b in up]),
        )
    done = []
    for _, dim in sides:
        low, high = edges[dim]
        around = [(width, width) if d in done else (0, 0) for d in range(value.ndim)]
        value = jnp.concatenate([jnp.pad(low, around), value, jnp.pad(high, around)], axis=dim)
        done.append(dim)
    return value


def extended(cells, sides, width):
    for axis, dim in sides:
        count = lax.axis_size(axis)
        head = lax.slice_in_dim(cells, 0, width, axis=dim)
        tail = lax.slice_in_dim(cells, cells.shape[dim] - width, cells.shape[dim], axis=dim)
        cells = jnp.concatenate(
            [
                lax.ppermute(tail, axis, [(i, (i + 1) % count) for i in range(count)]),
                cells,
                lax.ppermute(head, axis, [((i + 1) % count, i) for i in range(count)]),
            ],
            axis=dim,
        )
    return cells


def passed_along(value, axis, steps):
    count = lax.axis_size(axis)
    pairs = [(source, (source + steps) % count) for source in range(count)]
    return lax.ppermute(value, axis, pairs)


def cell_sides(slot_count):
    return (4.0 * spacing, 4.0 * spacing, spacing * (slot_count // 16))


def offset_list():
    chosen = []
    for step_z in (-1, 0, 1):
        for step_y in (-1, 0, 1):
            for step_x in (-1, 0, 1):
                forward = step_z > 0 or (
                    step_z == 0 and (step_y > 0 or (step_y == 0 and step_x >= 0))
                )
                if forward:
                    chosen.append((step_x, step_y, step_z))
    return chosen


def pair_terms(own_places, other_places, own_alive, other_alive, offset_vec, same_cell):
    shaped = jnp.asarray(offset_vec, own_places.dtype).reshape((3,) + (1,) * own_places.ndim)
    delta_vec = own_places[..., :, None] - (other_places[..., None, :] + shaped)
    distance = jnp.sum(delta_vec * delta_vec, axis=0)
    weight = own_alive[..., :, None] * other_alive[..., None, :]
    if same_cell:
        slot_count = own_places.shape[-1]
        rows_iota = lax.broadcasted_iota(jnp.int32, (slot_count, slot_count), 0)
        cols_iota = lax.broadcasted_iota(jnp.int32, (slot_count, slot_count), 1)
        weight = weight * (rows_iota != cols_iota).astype(weight.dtype)
    inside = jnp.where(distance < cut_radius * cut_radius, weight, jnp.zeros_like(weight))
    safe_sq = jnp.where(inside > 0.0, distance, jnp.ones_like(distance))
    inverse = 1.0 / safe_sq
    sixth_power = inverse * inverse * inverse
    magnitude = (
        24.0 * inverse * sixth_power * (2.0 * sixth_power - 1.0) - edge_force * lax.rsqrt(safe_sq)
    ) * inside
    pulled = delta_vec * magnitude
    return (jnp.sum(pulled, axis=-1), -jnp.sum(pulled, axis=-2))


def add_block(accumulated, piece, start):
    current = lax.dynamic_slice(accumulated, start, piece.shape)
    return lax.dynamic_update_slice(accumulated, current + piece, start)


def sweep_forces(padded, anchor, size_x, size_y, size_z, slot_count):
    cell_side = cell_sides(slot_count)
    block_depth = math.gcd(size_z, 2)
    chosen = offset_list()
    accumulated = jnp.zeros((3,) + padded.shape[1:], jnp.float32)

    def visit_block(block_index, accumulated):
        z_start = anchor + block_index * block_depth
        own_block = lax.dynamic_slice(
            padded, (0, 1, 1, z_start, 0), (4, size_x, size_y, block_depth, slot_count)
        )
        for step_x, step_y, step_z in chosen:
            side_block = lax.dynamic_slice(
                padded,
                (0, 1 + step_x, 1 + step_y, z_start + step_z, 0),
                (4, size_x, size_y, block_depth, slot_count),
            )
            same_cell = (step_x, step_y, step_z) == (0, 0, 0)
            offset_vec = (step_x * cell_side[0], step_y * cell_side[1], step_z * cell_side[2])
            near_term, far_term = pair_terms(
                own_block[:3], side_block[:3], own_block[3], side_block[3], offset_vec, same_cell
            )
            accumulated = add_block(accumulated, near_term, (0, 1, 1, z_start, 0))
            if not same_cell:
                accumulated = add_block(
                    accumulated, far_term, (0, 1 + step_x, 1 + step_y, z_start + step_z, 0)
                )
        return accumulated

    return lax.fori_loop(0, size_z // block_depth, visit_block, accumulated)


def per_device(places, velocity, forces_old, counts, mig_atom, mig_face):
    size_x, size_y, size_z, slot_count = places.shape[1:]
    cell_side = cell_sides(slot_count)
    alive_mask = (lax.broadcasted_iota(jnp.int32, places.shape[1:], 3) < counts[..., None]).astype(
        jnp.float32
    )
    half_velocity = velocity + 0.5 * step_size * forces_old
    drifted = places + step_size * half_velocity
    atom_ids = mig_atom.reshape(-1)
    face_ids = mig_face.reshape(-1)
    entries = atom_ids.shape[0]
    cell_id = atom_ids // slot_count
    pos_x = cell_id // (size_y * size_z)
    pos_y = cell_id // size_z % size_y
    pos_z = cell_id % size_z
    face_axis = face_ids // 2
    upward = face_ids % 2
    flat_places = drifted.reshape(3, -1)
    flat_velocity = half_velocity.reshape(3, -1)
    flat_alive = alive_mask.reshape(-1)
    along_axis = (lax.broadcasted_iota(jnp.int32, (3, entries), 0) == face_axis[None, :]).astype(
        jnp.float32
    )
    side_vec = jnp.asarray(cell_side, jnp.float32)[:, None]
    face_sign = (2 * upward - 1).astype(jnp.float32)
    carried = flat_places[:, atom_ids] - along_axis * face_sign[None, :] * side_vec
    new_x = jnp.where(face_axis == 0, (1 - upward) * (size_x - 1), pos_x)
    new_y = jnp.where(face_axis == 1, (1 - upward) * (size_y - 1), pos_y)
    new_z = jnp.where(face_axis == 2, (1 - upward) * (size_z - 1), pos_z)
    landing = ((new_x * size_y + new_y) * size_z + new_z).astype(jnp.float32)
    payload = jnp.concatenate([carried, flat_velocity[:, atom_ids], landing[None, :]], axis=0)
    empty_letter = jnp.concatenate(
        [jnp.zeros((6, entries), jnp.float32), -jnp.ones((1, entries), jnp.float32)], axis=0
    )
    letters = [
        jnp.where((face_ids == face_index)[None, :], payload, empty_letter)
        for face_index in range(6)
    ]
    flat_alive = flat_alive.at[atom_ids].set(0.0)
    message_box = jnp.zeros((2, 2, 2, 7, entries), jnp.float32)
    message_box = message_box.at[0, 0, 0].set(letters[0]).at[1, 0, 0].set(letters[1])
    message_box = message_box.at[0, 0, 1].set(letters[2]).at[0, 1, 1].set(letters[3])
    message_box = message_box.at[0, 1, 0].set(letters[4]).at[1, 1, 1].set(letters[5])
    opened = with_halo(message_box, (("gx", 0), ("gy", 1), ("gz", 2)), 1)
    arrivals = [
        opened[0, 1, 1],
        opened[3, 1, 1],
        opened[1, 0, 2],
        opened[1, 3, 2],
        opened[2, 2, 0],
        opened[1, 2, 3],
    ]
    inbound = jnp.concatenate(arrivals, axis=1)
    landing_ids = inbound[6].astype(jnp.int32)
    valid_entry = landing_ids >= 0
    inbound_total = inbound.shape[1]
    same_dest = (landing_ids[:, None] == landing_ids[None, :]) & valid_entry[None, :]
    earlier = lax.broadcasted_iota(
        jnp.int32, (inbound_total, inbound_total), 1
    ) < lax.broadcasted_iota(jnp.int32, (inbound_total, inbound_total), 0)
    arrival_rank = jnp.sum((same_dest & earlier).astype(jnp.int32), axis=1)
    safe_ids = jnp.where(valid_entry, landing_ids, 0)
    target = jnp.where(
        valid_entry,
        safe_ids * slot_count + counts.reshape(-1)[safe_ids] + arrival_rank,
        flat_alive.shape[0],
    )
    flat_places = flat_places.at[:, target].set(inbound[0:3], mode="drop")
    flat_velocity = flat_velocity.at[:, target].set(inbound[3:6], mode="drop")
    flat_alive = flat_alive.at[target].set(1.0, mode="drop")
    settled_places = flat_places.reshape(places.shape)
    settled_velocity = flat_velocity.reshape(places.shape)
    settled_alive = flat_alive.reshape(alive_mask.shape)
    full_state = jnp.concatenate([settled_places, settled_alive[None]], axis=0)
    cycle_cells = extended(full_state, (("gx", 1), ("gy", 2)), 1)
    above_layer = passed_along(cycle_cells[:, :, :, 0:1], "gz", -1)
    padded = jnp.concatenate([cycle_cells, above_layer], axis=3)
    accumulated = sweep_forces(padded, 0, size_x, size_y, size_z, slot_count)
    top_layer = passed_along(accumulated[:, :, :, size_z : size_z + 1], "gz", 1)
    accumulated = accumulated[:, :, :, :size_z].at[:, :, :, 0:1].add(top_layer)
    low_y = passed_along(accumulated[:, :, 0:1], "gy", -1)
    high_y = passed_along(accumulated[:, :, size_y + 1 : size_y + 2], "gy", 1)
    accumulated = (
        accumulated.at[:, :, size_y : size_y + 1]
        .add(low_y)
        .at[:, :, 1:2]
        .add(high_y)[:, :, 1 : size_y + 1]
    )
    low_x = passed_along(accumulated[:, 0:1], "gx", -1)
    high_x = passed_along(accumulated[:, size_x + 1 : size_x + 2], "gx", 1)
    new_force = (
        accumulated.at[:, size_x : size_x + 1].add(low_x).at[:, 1:2].add(high_x)[:, 1 : size_x + 1]
    )
    new_forces = new_force * settled_alive[None]
    new_velocity = (settled_velocity + 0.5 * step_size * new_forces) * settled_alive[None]
    new_places = settled_places * settled_alive[None]
    return (new_places, new_velocity, new_forces)


def solution(mesh):
    return jax.shard_map(
        per_device,
        mesh=mesh,
        in_specs=(
            P(None, "gx", "gy", "gz", None),
            P(None, "gx", "gy", "gz", None),
            P(None, "gx", "gy", "gz", None),
            P("gx", "gy", "gz"),
            P("gx", "gy", "gz", None),
            P("gx", "gy", "gz", None),
        ),
        out_specs=(
            P(None, "gx", "gy", "gz", None),
            P(None, "gx", "gy", "gz", None),
            P(None, "gx", "gy", "gz", None),
        ),
        check_vma=False,
    )
```

profile of v0, /device:TPU:1, one launch (start us, length us, event | category | flops | bytes accessed | tf_op | source)
XLA Modules:
  0.0 198.9 jit_solution(15156232223782145965)
XLA Ops:
  10.4 4.6 %collective-permute-start.5 = (f32[2,2,1,7,16]{4,3,2,1,0:T(8,128)S(1)}, f32[2,2,1,7,16]{4,3,2,1,0:T(8,128)S(1)}, u32[]{:S(2)}, u32[]{:S(2)}) collective-permute-start(f32[2,2,1,7,16]{4,3,2,1,0:T(8,128)S(1)} %get-tuple-element.743), channel_id=1, source_target_pairs={{1,0},{2,1},{3,2},{0,3},{5,4},{6,5},{7,6},{4,7},{9,8},{10,9},{11,1... | collective-permute-start | bytes 5384 | tf_op jit(solution)/shard_map/ppermute | solution.py:23
  15.1 4.9 %collective-permute-start.3 = (f32[2,1,2,7,16]{4,3,2,1,0:T(8,128)S(1)}, f32[2,1,2,7,16]{4,3,2,1,0:T(8,128)S(1)}, u32[]{:S(2)}, u32[]{:S(2)}) collective-permute-start(f32[2,1,2,7,16]{4,3,2,1,0:T(8,128)S(1)} %get-tuple-element.745), channel_id=1, source_target_pairs={{4,0},{8,4},{12,8},{16,12},{20,16},{24,20},{28,24},{32,28},{36,32}... | collective-permute-start | bytes 5384 | tf_op jit(solution)/shard_map/ppermute | solution.py:23
  22.3 3.6 %collective-permute-done.2 = f32[2,1,2,7,16]{4,3,2,1,0:T(8,128)S(1)} collective-permute-done((f32[2,1,2,7,16]{4,3,2,1,0:T(8,128)S(1)}, f32[2,1,2,7,16]{4,3,2,1,0:T(8,128)S(1)}, u32[]{:S(2)}, u32[]{:S(2)}) %collective-permute-start.2) | collective-permute-done | bytes 1824 | tf_op jit(solution)/shard_map/ppermute | solution.py:22
  37.0 3.4 %collective-permute-done.9 = f32[4,8,1,6,128]{4,3,1,2,0:T(8,128)S(1)} collective-permute-done((f32[4,8,1,6,128]{4,3,1,2,0:T(8,128)S(1)}, f32[4,8,1,6,128]{4,3,1,2,0:T(8,128)S(1)}, u32[]{:S(2)}, u32[]{:S(2)}) %collective-permute-start.9) | collective-permute-done | bytes 98336 | tf_op jit(solution)/shard_map/ppermute | solution.py:43
  40.4 3.2 %collective-permute-done.8 = f32[4,8,1,6,128]{4,3,1,2,0:T(8,128)S(1)} collective-permute-done((f32[4,8,1,6,128]{4,3,1,2,0:T(8,128)S(1)}, f32[4,8,1,6,128]{4,3,1,2,0:T(8,128)S(1)}, u32[]{:S(2)}, u32[]{:S(2)}) %collective-permute-start.8) | collective-permute-done | bytes 98336 | tf_op jit(solution)/shard_map/ppermute | solution.py:41
  43.6 3.0 %collective-permute-start.10 = (f32[4,8,3,1,128]{4,3,1,2,0:T(1,128)S(1)}, f32[4,8,3,1,128]{4,3,1,2,0:T(1,128)S(1)}, u32[]{:S(2)}, u32[]{:S(2)}) collective-permute-start(f32[4,8,3,1,128]{4,3,1,2,0:T(1,128)S(1)} %pad_maximum_fusion.2), channel_id=1, source_target_pairs={{0,3},{1,0},{2,1},{3,2},{4,7},{5,4},{6,5},{7,6},{8,11},{9,8},{10,9... | collective-permute-start | bytes 147464 | tf_op jit(solution)/shard_map/ppermute | solution.py:53
  47.9 127.1 %while.28 = (s32[]{:T(128)}, f32[3,8,3,7,128]{4,3,1,0,2:T(8,128)S(1)}, f32[4,8,3,7,128]{4,3,1,2,0:T(8,128)S(1)}, s32[]{:T(128)}, s32[]{:T(128)}, /*index=5*/s32[...) while((s32[]{:T(128)}, ...), condition=%wide.region_47.48_spmd.clone, body=%wide.region_5.47_spmd.sunk.clone.sunk | while | flops 98849800 | bytes 65160536 | solution.py:128
  52.6 8.6 %fusion.115 = (f32[3,6,2,128]{3,2,1,0:T(2,128)}, f32[3,6,2,128]{3,2,1,0:T(2,128)}, f32[6,2,128,128]{3,2,1,0:T(8,128)S(1)}, f32[6,2,128,128]{3,2,1,0:T(8,128)S(1)...) fusion(f32[6,2,128,128]{3,2,1,0:T(8,128)S(1)} %get-tuple-elemen, ...), kind=kLoop, calls=%fused_computation.59.clone.1 | loop fusion | flops 23766528 | bytes 11360256 | tf_op jit(solution)/shard_map/while/body/eval_jaxpr/reduce_sum | solution.py:91
  67.1 2.5 %subtract_multiply_fusion.46 = (f32[6,2,128,128]{3,2,1,0:T(8,128)S(1)}, f32[6,2,128,128]{3,2,1,0:T(8,128)S(1)}) fusion(f32[6,2,128,128]{3,2,1,0:T(8,128)} %get-tuple-element.886, f32[6,2,128]{2,1,0:T(2,128)} %get-tuple-element.887, f32[6,2,128]{2,1,0:T(2,128)S(1)} %get-tuple-element.864, f32[6,2,128,128]{3,2,1,0:T(8,128)} %get-tuple-element.888, ...), kind=kLoop, calls=%fused_computation.96.clone.1 | loop fusion | flops 6291456 | bytes 3164160 | tf_op jit(solution)/shard_map/while/body/eval_jaxpr/mul | solution.py:87
  69.7 5.4 %subtract_multiply_fusion.47 = (f32[6,2,128,128]{3,2,1,0:T(8,128)S(1)}, f32[6,2,128,128]{3,2,1,0:T(8,128)S(1)}, f32[6,2,128,128]{3,2,1,0:T(8,128)S(1)}, f32[6,2,...) fusion(f32[6,2,128,128]{3,2,1,0:T(8,128)} %get-tuple-element.89, ...), kind=kLoop, calls=%fused_computation.99.clone.1 | loop fusion | flops 28311552 | bytes 14217216 | tf_op jit(solution)/shard_map/while/body/eval_jaxpr/mul | solution.py:87
  75.2 2.5 %fusion.117 = (f32[3,6,2,128]{3,2,1,0:T(2,128)S(1)}, f32[3,6,2,128]{3,2,1,0:T(2,128)S(1)}, f32[3,6,2,128]{3,2,1,0:T(2,128)S(1)}, f32[3,6,2,128]{3,2,1,0:T(2,128)S(1)}) fusion(f32[6,2,128,128]{3,2,1,0:T(8,128)S(1)} %get-tuple-element.933, f32[3,6,2,128]{3,2,1,0:T(2,128)S(1)} %copy-done.21, f32[3,6,2,128]{3,2,1,0:T(2,128)S(1)} %dynamic-slice_bitcast_fusion.15, ...), kind=kLoop, calls=%fused_computation.55.clone.1 | loop fusion | flops 4700160 | bytes 1701888 | tf_op jit(solution)/shard_map/while/body/eval_jaxpr/reduce_sum | solution.py:91
  77.8 7.6 %fusion.116 = (f32[3,6,2,128]{3,2,1,0:T(2,128)S(1)}, f32[3,6,2,128]{3,2,1,0:T(2,128)S(1)}, f32[3,6,2,128]{3,2,1,0:T(2,128)S(1)}, f32[3,6,2,128]{3,2,1,0:T(2,128)...) fusion(f32[6,2,128,128]{3,2,1,0:T(8,128)S(1)} %get-tuple-elemen, ...), kind=kLoop, calls=%fused_computation.57.clone.1 | loop fusion | flops 21150720 | bytes 7593984 | tf_op jit(solution)/shard_map/while/body/eval_jaxpr/reduce_sum | solution.py:91
  94.9 8.6 %fusion.115 = (f32[3,6,2,128]{3,2,1,0:T(2,128)}, f32[3,6,2,128]{3,2,1,0:T(2,128)}, f32[6,2,128,128]{3,2,1,0:T(8,128)S(1)}, f32[6,2,128,128]{3,2,1,0:T(8,128)S(1)...) fusion(f32[6,2,128,128]{3,2,1,0:T(8,128)S(1)} %get-tuple-elemen, ...), kind=kLoop, calls=%fused_computation.59.clone.1 | loop fusion | flops 23766528 | bytes 11360256 | tf_op jit(solution)/shard_map/while/body/eval_jaxpr/reduce_sum | solution.py:91
  112.0 5.4 %subtract_multiply_fusion.47 = (f32[6,2,128,128]{3,2,1,0:T(8,128)S(1)}, f32[6,2,128,128]{3,2,1,0:T(8,128)S(1)}, f32[6,2,128,128]{3,2,1,0:T(8,128)S(1)}, f32[6,2,...) fusion(f32[6,2,128,128]{3,2,1,0:T(8,128)} %get-tuple-element.89, ...), kind=kLoop, calls=%fused_computation.99.clone.1 | loop fusion | flops 28311552 | bytes 14217216 | tf_op jit(solution)/shard_map/while/body/eval_jaxpr/mul | solution.py:87
  117.5 2.5 %fusion.117 = (f32[3,6,2,128]{3,2,1,0:T(2,128)S(1)}, f32[3,6,2,128]{3,2,1,0:T(2,128)S(1)}, f32[3,6,2,128]{3,2,1,0:T(2,128)S(1)}, f32[3,6,2,128]{3,2,1,0:T(2,128)S(1)}) fusion(f32[6,2,128,128]{3,2,1,0:T(8,128)S(1)} %get-tuple-element.933, f32[3,6,2,128]{3,2,1,0:T(2,128)S(1)} %copy-done.21, f32[3,6,2,128]{3,2,1,0:T(2,128)S(1)} %dynamic-slice_bitcast_fusion.15, ...), kind=kLoop, calls=%fused_computation.55.clone.1 | loop fusion | flops 4700160 | bytes 1701888 | tf_op jit(solution)/shard_map/while/body/eval_jaxpr/reduce_sum | solution.py:91
  120.1 7.6 %fusion.116 = (f32[3,6,2,128]{3,2,1,0:T(2,128)S(1)}, f32[3,6,2,128]{3,2,1,0:T(2,128)S(1)}, f32[3,6,2,128]{3,2,1,0:T(2,128)S(1)}, f32[3,6,2,128]{3,2,1,0:T(2,128)...) fusion(f32[6,2,128,128]{3,2,1,0:T(8,128)S(1)} %get-tuple-elemen, ...), kind=kLoop, calls=%fused_computation.57.clone.1 | loop fusion | flops 21150720 | bytes 7593984 | tf_op jit(solution)/shard_map/while/body/eval_jaxpr/reduce_sum | solution.py:91
  137.3 8.6 %fusion.115 = (f32[3,6,2,128]{3,2,1,0:T(2,128)}, f32[3,6,2,128]{3,2,1,0:T(2,128)}, f32[6,2,128,128]{3,2,1,0:T(8,128)S(1)}, f32[6,2,128,128]{3,2,1,0:T(8,128)S(1)...) fusion(f32[6,2,128,128]{3,2,1,0:T(8,128)S(1)} %get-tuple-elemen, ...), kind=kLoop, calls=%fused_computation.59.clone.1 | loop fusion | flops 23766528 | bytes 11360256 | tf_op jit(solution)/shard_map/while/body/eval_jaxpr/reduce_sum | solution.py:91
  151.7 2.5 %subtract_multiply_fusion.46 = (f32[6,2,128,128]{3,2,1,0:T(8,128)S(1)}, f32[6,2,128,128]{3,2,1,0:T(8,128)S(1)}) fusion(f32[6,2,128,128]{3,2,1,0:T(8,128)} %get-tuple-element.886, f32[6,2,128]{2,1,0:T(2,128)} %get-tuple-element.887, f32[6,2,128]{2,1,0:T(2,128)S(1)} %get-tuple-element.864, f32[6,2,128,128]{3,2,1,0:T(8,128)} %get-tuple-element.888, ...), kind=kLoop, calls=%fused_computation.96.clone.1 | loop fusion | flops 6291456 | bytes 3164160 | tf_op jit(solution)/shard_map/while/body/eval_jaxpr/mul | solution.py:87
  154.3 5.4 %subtract_multiply_fusion.47 = (f32[6,2,128,128]{3,2,1,0:T(8,128)S(1)}, f32[6,2,128,128]{3,2,1,0:T(8,128)S(1)}, f32[6,2,128,128]{3,2,1,0:T(8,128)S(1)}, f32[6,2,...) fusion(f32[6,2,128,128]{3,2,1,0:T(8,128)} %get-tuple-element.89, ...), kind=kLoop, calls=%fused_computation.99.clone.1 | loop fusion | flops 28311552 | bytes 14217216 | tf_op jit(solution)/shard_map/while/body/eval_jaxpr/mul | solution.py:87
  159.8 2.5 %fusion.117 = (f32[3,6,2,128]{3,2,1,0:T(2,128)S(1)}, f32[3,6,2,128]{3,2,1,0:T(2,128)S(1)}, f32[3,6,2,128]{3,2,1,0:T(2,128)S(1)}, f32[3,6,2,128]{3,2,1,0:T(2,128)S(1)}) fusion(f32[6,2,128,128]{3,2,1,0:T(8,128)S(1)} %get-tuple-element.933, f32[3,6,2,128]{3,2,1,0:T(2,128)S(1)} %copy-done.21, f32[3,6,2,128]{3,2,1,0:T(2,128)S(1)} %dynamic-slice_bitcast_fusion.15, ...), kind=kLoop, calls=%fused_computation.55.clone.1 | loop fusion | flops 4700160 | bytes 1701888 | tf_op jit(solution)/shard_map/while/body/eval_jaxpr/reduce_sum | solution.py:91
  162.4 7.6 %fusion.116 = (f32[3,6,2,128]{3,2,1,0:T(2,128)S(1)}, f32[3,6,2,128]{3,2,1,0:T(2,128)S(1)}, f32[3,6,2,128]{3,2,1,0:T(2,128)S(1)}, f32[3,6,2,128]{3,2,1,0:T(2,128)...) fusion(f32[6,2,128,128]{3,2,1,0:T(8,128)S(1)} %get-tuple-elemen, ...), kind=kLoop, calls=%fused_computation.57.clone.1 | loop fusion | flops 21150720 | bytes 7593984 | tf_op jit(solution)/shard_map/while/body/eval_jaxpr/reduce_sum | solution.py:91
  175.7 4.4 %collective-permute-done.11 = f32[3,8,3,1,128]{4,2,3,1,0:T(4,128)S(1)} collective-permute-done((f32[3,8,3,1,128]{4,2,3,1,0:T(4,128)S(1)}, f32[3,8,3,1,128]{4,2,3,1,0:T(4,128)S(1)}, u32[]{:S(2)}, u32[]{:S(2)}) %collective-permute-start.11) | collective-permute-done | bytes 36896 | tf_op jit(solution)/shard_map/ppermute | solution.py:53
  183.5 3.6 %collective-permute-done.13 = f32[3,8,1,6,128]{4,2,3,1,0:T(1,128)S(1)} collective-permute-done((f32[3,8,1,6,128]{4,2,3,1,0:T(1,128)S(1)}, f32[3,8,1,6,128]{4,2,3,1,0:T(1,128)S(1)}, u32[]{:S(2)}, u32[]{:S(2)}) %collective-permute-start.13) | collective-permute-done | bytes 73760 | tf_op jit(solution)/shard_map/ppermute | solution.py:53
  187.2 4.7 %collective-permute-start.14 = (f32[3,1,1,6,128]{4,2,3,1,0:T(1,128)S(1)}, f32[3,1,1,6,128]{4,2,3,1,0:T(1,128)S(1)}, u32[]{:S(2)}, u32[]{:S(2)}) collective-permute-start(f32[3,1,1,6,128]{4,2,3,1,0:T(1,128)S(1)} %slice.914), channel_id=1, source_target_pairs={{0,64},{64,0},{1,65},{65,1},{2,66},{66,2},{3,67},{67,3},{4,68},{68... | collective-permute-start | bytes 27656 | tf_op jit(solution)/shard_map/ppermute | solution.py:53
  (435 shorter events, 82.3 us)
Async XLA Ops:
  4.4 16.9 %copy-start.28 = (s32[6,1,6]{2,1,0:T(1,128)S(1)}, s32[6,1,6]{2,1,0:T(1,128)}, u32[]{:S(2)}) copy-start(s32[6,1,6]{2,1,0:T(1,128)} %param.48) | copy-start | bytes 436
  10.4 11.7 %collective-permute-start.5 = (f32[2,2,1,7,16]{4,3,2,1,0:T(8,128)S(1)}, f32[2,2,1,7,16]{4,3,2,1,0:T(8,128)S(1)}, u32[]{:S(2)}, u32[]{:S(2)}) collective-permute-start(f32[2,2,1,7,16]{4,3,2,1,0:T(8,128)S(1)} %get-tuple-element.743), channel_id=1, source_target_pairs={{1,0},{2,1},{3,2},{0,3},{5,4},{6,5},{7,6},{4,7},{9,8},{10,9},{11,1... | collective-permute-start | bytes 5384 | tf_op jit(solution)/shard_map/ppermute | solution.py:23
  15.1 7.2 %collective-permute-start.4 = (f32[2,2,1,7,16]{4,3,2,1,0:T(8,128)S(1)}, f32[2,2,1,7,16]{4,3,2,1,0:T(8,128)S(1)}, u32[]{:S(2)}, u32[]{:S(2)}) collective-permute-start(f32[2,2,1,7,16]{4,3,2,1,0:T(8,128)S(1)} %get-tuple-element.744), channel_id=1, source_target_pairs={{0,1},{1,2},{2,3},{3,0},{4,5},{5,6},{6,7},{7,4},{8,9},{9,10},{10,1... | collective-permute-start | bytes 5384 | tf_op jit(solution)/shard_map/ppermute | solution.py:22
  15.1 7.2 %collective-permute-start.3 = (f32[2,1,2,7,16]{4,3,2,1,0:T(8,128)S(1)}, f32[2,1,2,7,16]{4,3,2,1,0:T(8,128)S(1)}, u32[]{:S(2)}, u32[]{:S(2)}) collective-permute-start(f32[2,1,2,7,16]{4,3,2,1,0:T(8,128)S(1)} %get-tuple-element.745), channel_id=1, source_target_pairs={{4,0},{8,4},{12,8},{16,12},{20,16},{24,20},{28,24},{32,28},{36,32}... | collective-permute-start | bytes 5384 | tf_op jit(solution)/shard_map/ppermute | solution.py:23
  20.0 5.9 %collective-permute-start.2 = (f32[2,1,2,7,16]{4,3,2,1,0:T(8,128)S(1)}, f32[2,1,2,7,16]{4,3,2,1,0:T(8,128)S(1)}, u32[]{:S(2)}, u32[]{:S(2)}) collective-permute-start(f32[2,1,2,7,16]{4,3,2,1,0:T(8,128)S(1)} %get-tuple-element.746), channel_id=1, source_target_pairs={{0,4},{4,8},{8,12},{12,16},{16,20},{20,24},{24,28},{28,32},{32,36}... | collective-permute-start | bytes 5384 | tf_op jit(solution)/shard_map/ppermute | solution.py:22
  20.0 5.9 %collective-permute-start.1 = (f32[1,2,2,7,16]{4,3,2,1,0:T(8,128)S(1)}, f32[1,2,2,7,16]{4,3,2,1,0:T(8,128)S(1)}, u32[]{:S(2)}, u32[]{:S(2)}) collective-permute-start(f32[1,2,2,7,16]{4,3,2,1,0:T(8,128)S(1)} %get-tuple-element.747), channel_id=1, source_target_pairs={{64,0},{0,64},{65,1},{1,65},{66,2},{2,66},{67,3},{3,67},{68,4},{4,... | collective-permute-start | bytes 5384 | tf_op jit(solution)/shard_map/ppermute | solution.py:23
  22.1 3.8 %collective-permute-start = (f32[1,2,2,7,16]{4,3,2,1,0:T(8,128)S(1)}, f32[1,2,2,7,16]{4,3,2,1,0:T(8,128)S(1)}, u32[]{:S(2)}, u32[]{:S(2)}) collective-permute-start(f32[1,2,2,7,16]{4,3,2,1,0:T(8,128)S(1)} %get-tuple-element.748), channel_id=1, source_target_pairs={{0,64},{64,0},{1,65},{65,1},{2,66},{66,2},{3,67},{67,3},{4,68},{68... | collective-permute-start | bytes 5384 | tf_op jit(solution)/shard_map/ppermute | solution.py:22
  28.1 19.7 %copy-start.29 = (s32[96]{0:T(128)}, s32[96]{0:T(128)S(1)}, u32[]{:S(2)}) copy-start(s32[96]{0:T(128)S(1)} %fusion.98) | copy-start | bytes 1156
  30.8 17.0 %copy-start.4 = (f32[3,4608]{0,1:T(8,128)}, f32[3,4608]{0,1:T(8,128)S(1)}, u32[]{:S(2)}) copy-start(f32[3,4608]{0,1:T(8,128)S(1)} %scatter_fusion) | copy-start | bytes 165892
  31.8 3.3 %collective-permute-start.6 = (f32[4,1,1,6,128]{4,3,1,2,0:T(8,128)S(1)}, f32[4,1,1,6,128]{4,3,1,2,0:T(8,128)S(1)}, u32[]{:S(2)}, u32[]{:S(2)}) collective-permute-start(f32[4,1,1,6,128]{4,3,1,2,0:T(8,128)S(1)} %get-tuple-element.739), channel_id=1, source_target_pairs={{0,64},{64,0},{1,65},{65,1},{2,66},{66,2},{3,67},{67,3},{4,68},{68... | collective-permute-start | bytes 36872 | tf_op jit(solution)/shard_map/ppermute | solution.py:41
  34.2 1.2 collective-permute-start.7
  35.4 5.0 %collective-permute-start.9 = (f32[4,8,1,6,128]{4,3,1,2,0:T(8,128)S(1)}, f32[4,8,1,6,128]{4,3,1,2,0:T(8,128)S(1)}, u32[]{:S(2)}, u32[]{:S(2)}) collective-permute-start(f32[4,8,1,6,128]{4,3,1,2,0:T(8,128)S(1)} %pad_maximum_fusion.1), channel_id=1, source_target_pairs={{4,0},{8,4},{12,8},{16,12},{20,16},{24,20},{28,24},{32,28},{36,32}... | collective-permute-start | bytes 294920 | tf_op jit(solution)/shard_map/ppermute | solution.py:43
  35.8 7.8 %collective-permute-start.8 = (f32[4,8,1,6,128]{4,3,1,2,0:T(8,128)S(1)}, f32[4,8,1,6,128]{4,3,1,2,0:T(8,128)S(1)}, u32[]{:S(2)}, u32[]{:S(2)}) collective-permute-start(f32[4,8,1,6,128]{4,3,1,2,0:T(8,128)S(1)} %pad_maximum_fusion.1), channel_id=1, source_target_pairs={{0,4},{4,8},{8,12},{12,16},{16,20},{20,24},{24,28},{28,32},{32,36}... | collective-permute-start | bytes 294920 | tf_op jit(solution)/shard_map/ppermute | solution.py:41
  43.6 4.2 %collective-permute-start.10 = (f32[4,8,3,1,128]{4,3,1,2,0:T(1,128)S(1)}, f32[4,8,3,1,128]{4,3,1,2,0:T(1,128)S(1)}, u32[]{:S(2)}, u32[]{:S(2)}) collective-permute-start(f32[4,8,3,1,128]{4,3,1,2,0:T(1,128)S(1)} %pad_maximum_fusion.2), channel_id=1, source_target_pairs={{0,3},{1,0},{2,1},{3,2},{4,7},{5,4},{6,5},{7,6},{8,11},{9,8},{10,9... | collective-permute-start | bytes 147464 | tf_op jit(solution)/shard_map/ppermute | solution.py:53
  77.8 12.7 %copy-start.6 = (f32[4,8,3,7,128]{4,3,1,2,0:T(8,128)S(1)}, f32[4,8,3,7,128]{4,3,1,2,0:T(8,128)}, u32[]{:S(2)}) copy-start(f32[4,8,3,7,128]{4,3,1,2,0:T(8,128)} %copy-done.5) | copy-start | bytes 1032196 | tf_op jit(solution)/shard_map/while
  120.1 12.7 %copy-start.6 = (f32[4,8,3,7,128]{4,3,1,2,0:T(8,128)S(1)}, f32[4,8,3,7,128]{4,3,1,2,0:T(8,128)}, u32[]{:S(2)}) copy-start(f32[4,8,3,7,128]{4,3,1,2,0:T(8,128)} %copy-done.5) | copy-start | bytes 1032196 | tf_op jit(solution)/shard_map/while
  175.1 20.5 %copy-start.31 = (f32[96,3]{0,1:T(4,128)S(1)}, f32[96,3]{0,1:T(4,128)}, u32[]{:S(2)}) copy-start(f32[96,3]{0,1:T(4,128)} %get-tuple-element.750) | copy-start | bytes 3460
  175.1 20.6 %copy-start.7 = (f32[3,6,1,6,128]{0,4,3,1,2:T(8,128)S(1)}, f32[3,6,1,6,128]{0,4,3,1,2:T(8,128)}, u32[]{:S(2)}) copy-start(f32[3,6,1,6,128]{0,4,3,1,2:T(8,128)} %copy.51) | copy-start | bytes 165892
  175.1 20.6 %copy-start.30 = (s32[96]{0:T(128)S(1)}, s32[96]{0:T(128)}, u32[]{:S(2)}) copy-start(s32[96]{0:T(128)} %copy-done.29) | copy-start | bytes 1156
  175.3 4.7 %collective-permute-start.11 = (f32[3,8,3,1,128]{4,2,3,1,0:T(4,128)S(1)}, f32[3,8,3,1,128]{4,2,3,1,0:T(4,128)S(1)}, u32[]{:S(2)}, u32[]{:S(2)}) collective-permute-start(f32[3,8,3,1,128]{4,2,3,1,0:T(4,128)S(1)} %slice.909), channel_id=1, source_target_pairs={{0,1},{1,2},{2,3},{3,0},{4,5},{5,6},{6,7},{7,4},{8,9},{9,10},{10,1... | collective-permute-start | bytes 110600 | tf_op jit(solution)/shard_map/ppermute | solution.py:53
  180.2 3.3 %collective-permute-start.12 = (f32[3,8,1,6,128]{4,2,3,1,0:T(1,128)S(1)}, f32[3,8,1,6,128]{4,2,3,1,0:T(1,128)S(1)}, u32[]{:S(2)}, u32[]{:S(2)}) collective-permute-start(f32[3,8,1,6,128]{4,2,3,1,0:T(1,128)S(1)} %get-tuple-element.737), channel_id=1, source_target_pairs={{0,60},{4,0},{8,4},{12,8},{16,12},{20,16},{24,20},{28,24},{32,28},... | collective-permute-start | bytes 221192 | tf_op jit(solution)/shard_map/ppermute | solution.py:53
  180.5 6.5 %collective-permute-start.13 = (f32[3,8,1,6,128]{4,2,3,1,0:T(1,128)S(1)}, f32[3,8,1,6,128]{4,2,3,1,0:T(1,128)S(1)}, u32[]{:S(2)}, u32[]{:S(2)}) collective-permute-start(f32[3,8,1,6,128]{4,2,3,1,0:T(1,128)S(1)} %get-tuple-element.738), channel_id=1, source_target_pairs={{0,4},{4,8},{8,12},{12,16},{16,20},{20,24},{24,28},{28,32},{32,36}... | collective-permute-start | bytes 221192 | tf_op jit(solution)/shard_map/ppermute | solution.py:53
  187.2 5.6 %collective-permute-start.14 = (f32[3,1,1,6,128]{4,2,3,1,0:T(1,128)S(1)}, f32[3,1,1,6,128]{4,2,3,1,0:T(1,128)S(1)}, u32[]{:S(2)}, u32[]{:S(2)}) collective-permute-start(f32[3,1,1,6,128]{4,2,3,1,0:T(1,128)S(1)} %slice.914), channel_id=1, source_target_pairs={{0,64},{64,0},{1,65},{65,1},{2,66},{66,2},{3,67},{67,3},{4,68},{68... | collective-permute-start | bytes 27656 | tf_op jit(solution)/shard_map/ppermute | solution.py:53
  192.8 5.3 %collective-permute-start.15 = (f32[3,1,1,6,128]{4,2,3,1,0:T(1,128)S(1)}, f32[3,1,1,6,128]{4,2,3,1,0:T(1,128)S(1)}, u32[]{:S(2)}, u32[]{:S(2)}) collective-permute-start(f32[3,1,1,6,128]{4,2,3,1,0:T(1,128)S(1)} %get-tuple-element.741), channel_id=1, source_target_pairs={{0,64},{64,0},{1,65},{65,1},{2,66},{66,2},{3,67},{67,3},{4,68},{68... | collective-permute-start | bytes 27656 | tf_op jit(solution)/shard_map/ppermute | solution.py:53
  (72 other events, 384.4 us)
where the time goes:
time: 200 us; the launch traced here: 199 us
  other arithmetic  107 us (54%)
  local copies, waits for them, and re-layouts  40 us (20%)
  starting transfers between devices  25 us (12%)
  waiting for transfers between devices  23.1 us (12%)
  loops' own time  2.76 us (1%)
    reduce_sum x9, other arithmetic, pair_terms(): return (jnp.sum(pulled, axis=-1), -jnp.sum(pulled, axis=-2))  56 us
    mul x9, other arithmetic, pair_terms(): (24.0 * inverse * sixth_power * (2.0 * sixth_power - 1.0) - edge_force *...  28.3 us
    dynamic_update_slice x81, local copies, waits for them, and re-layouts, add_block(): return lax.dynamic_update_slice(accumulated, current + piece, start)  20.1 us
    ppermute x6, waiting for transfers between devices, passed_along(): return lax.ppermute(value, axis, pairs)  11.7 us
    add x81, other arithmetic, add_block(): return lax.dynamic_update_slice(accumulated, current + piece, start)  11.3 us
    ppermute x3, starting transfers between devices, with_halo(): lax.ppermute(initial, axis, [(b, a) for a, b in up])  10.8 us
    ppermute x6, starting transfers between devices, passed_along(): return lax.ppermute(value, axis, pairs)  10 us
  transfers between devices with their start and end apart: 16, of which 10 were waited for; matrix products, arithmetic and copies ran while one was open for 3% of the time, Pallas kernels for 0%

commit v1 on v0

v1 whole, which is shorter than its diff:
```python
import functools

import jax
import jax.numpy as jnp
from jax import lax
from jax.experimental import pallas as pl
from jax.experimental.pallas import tpu as pltpu
from jax.sharding import PartitionSpec as P

MESH = pl.DeviceIdType.MESH
F32 = jnp.float32
I32 = jnp.int32
STEP = 0.005
RC = 2.5
SPACING = 1.1
EDGE = 24.0 * (2.0 * RC ** (-13) - RC ** (-7))
SIDE = (4.0 * SPACING, 4.0 * SPACING, SPACING * 8)
FAR = 1.0e4
REACH = RC * 1.0005
SX, SZ, CAP, MIG = 6, 6, 128, 16
NDIR = 27
ROWS = 4
NL = 2
NT = 32


def iota(shape, dim):
    return lax.broadcasted_iota(I32, shape, dim)


def exchange_kernel(sizes, counts, atoms, faces, places, velocity, forces,
                    own, vel, yblk, slab, zrow,
                    drift, half, letter, inbox, zsend,
                    lsend, lrecv, bsend, brecv, ssend, srecv, zs, zr):
    n_gx, n_gy, n_gz = sizes
    me = (lax.axis_index("gx"), lax.axis_index("gy"), lax.axis_index("gz"))

    def at(dx, dy, dz):
        return (
            lax.rem(me[0] + dx + n_gx, n_gx),
            lax.rem(me[1] + dy + n_gy, n_gy),
            lax.rem(me[2] + dz + n_gz, n_gz),
        )

    barrier = pltpu.get_barrier_semaphore()
    around = [
        (dx, dy, dz) for dx in (0, 1) for dy in (-1, 0, 1) for dz in (-1, 0, 1) if (dx, dy, dz) != (0, 0, 0)
    ]
    for step in around:
        pl.semaphore_signal(barrier, inc=1, device_id=at(*step), device_id_type=MESH)

    for c in range(3):
        for x in range(SX):
            h = velocity[c, x] + 0.5 * STEP * forces[c, x]
            half[c, x] = h
            drift[c, x] = places[c, x] + STEP * h

    sub8 = iota((8, CAP), 0)
    lane8 = iota((8, CAP), 1)
    lane1 = iota((1, CAP), 1)
    out_letter = jnp.where(sub8 == 6, -1.0, 0.0).astype(F32)
    leaving_cell = jnp.full((1, CAP), -1.0, F32)
    leaving_slot = jnp.full((1, CAP), -1.0, F32)
    for k in range(MIG):
        atom = atoms[0, 0, 0, k]
        face = faces[0, 0, 0, k]
        cell = lax.shift_right_logical(atom, 7)
        slot = atom & 127
        cx = lax.div(cell, SZ)
        cz = lax.rem(cell, SZ)
        axis = lax.shift_right_logical(face, 1)
        up = face & 1
        tile = jnp.zeros((8, CAP), F32)
        for c in range(6):
            source = drift if c < 3 else half
            row = source[c % 3, cx, pl.ds(cz, 1), :]
            tile = jnp.where(sub8 == c, jnp.broadcast_to(row, (8, CAP)), tile)
        column = jnp.sum(jnp.where(lane8 == slot, tile, 0.0), axis=1, keepdims=True)
        sign = (2 * up - 1).astype(F32)
        shift = jnp.where(axis == 2, SIDE[2], SIDE[0]).astype(F32) * sign
        sub_col = iota((8, 1), 0)
        column = column - jnp.where(sub_col == axis, shift, 0.0)
        nx = jnp.where(axis == 0, (1 - up) * (SX - 1), cx)
        nz = jnp.where(axis == 2, (1 - up) * (SZ - 1), cz)
        column = jnp.where(sub_col == 6, (nx * 8 + nz).astype(F32), column)
        out_letter = jnp.where(lane8 == 16 * (face ^ 1) + k, column, out_letter)
        leaving_cell = jnp.where(lane1 == 96 + k, (cx * 8 + cz).astype(F32), leaving_cell)
        leaving_slot = jnp.where(lane1 == 96 + k, slot.astype(F32), leaving_slot)
    letter[...] = out_letter

    pl.semaphore_wait(barrier, len(around))

    posts = []
    for box, step in enumerate(((1, 0, 0), (0, 1, 0), (0, -1, 0), (0, 0, 1), (0, 0, -1))):
        post = pltpu.make_async_remote_copy(
            src_ref=letter, dst_ref=inbox.at[box], send_sem=lsend.at[box], recv_sem=lrecv.at[box],
            device_id=at(*step), device_id_type=MESH,
        )
        post.start()
        posts.append(post)

    count_rows = []
    for x in range(SX):
        row = jnp.zeros((8, CAP), I32)
        for z in range(SZ):
            row = jnp.where(sub8 == z, counts[x, 0, z], row)
        count_rows.append(row)

    for post in posts:
        post.wait_recv()
    got = inbox[4]
    for box, top in ((3, 80), (2, 64), (1, 48), (0, 32)):
        got = jnp.where(lane8 < top, inbox[box], got)
    arriving_cell = jnp.where(lane1 < 96, got[6:7, :], -1.0)
    sub8f = sub8.astype(F32)
    here = []
    gone = []
    for x in range(SX):
        here.append((jnp.broadcast_to(arriving_cell, (8, CAP)) == sub8f + 8.0 * x).astype(F32))
        gone.append((jnp.broadcast_to(leaving_cell, (8, CAP)) == sub8f + 8.0 * x).astype(F32))
    here_all = jnp.concatenate(here, axis=0)
    gone_all = jnp.concatenate(gone, axis=0)
    earlier = (iota((CAP, CAP), 0) < iota((CAP, CAP), 1)).astype(jnp.bfloat16)
    rank = jnp.dot(here_all.astype(jnp.bfloat16), earlier, preferred_element_type=F32)
    slot_table = here_all * (rank + jnp.concatenate(count_rows, axis=0).astype(F32))
    target = jnp.sum(slot_table, axis=0, keepdims=True)
    target = jnp.where(lane1 < 96, target, leaving_slot)
    slot_hit = (jnp.broadcast_to(target, (CAP, CAP)) == iota((CAP, CAP), 0).astype(F32)).astype(jnp.bfloat16)
    pieces = [(here_all - gone_all).astype(jnp.bfloat16)]
    for c in range(6):
        part = here_all * jnp.broadcast_to(jnp.where(lane1 < 96, got[c : c + 1, :], 0.0), here_all.shape)
        for _ in range(3):
            top = part.astype(jnp.bfloat16)
            pieces.append(top)
            part = part - top.astype(F32)
    landed = lax.dot_general(
        jnp.concatenate(pieces, axis=0), slot_hit, (((1,), (1,)), ((), ())), preferred_element_type=F32
    )
    n = SX * 8

    def arrived(c, x):
        base = n * (1 + 3 * c) + 8 * x
        return (
            landed[base : base + SZ] + landed[base + n : base + n + SZ] + landed[base + 2 * n : base + 2 * n + SZ]
        )

    lane6 = iota((SZ, CAP), 1)
    for x in range(SX):
        delta = landed[8 * x : 8 * x + SZ]
        live = (lane6 < count_rows[x][:SZ]).astype(F32) + delta > 0.5
        came = delta > 0.5
        for c in range(3):
            place = jnp.where(came, arrived(c, x), drift[c, x])
            place = jnp.where(live, place, FAR)
            own[c, x, 0:SZ] = place
            own[c, x, SZ:8] = jnp.full((8 - SZ, CAP), FAR, F32)
            zsend[0, c, x : x + 1] = place[0:1]
            zsend[1, c, x : x + 1] = place[SZ - 1 : SZ]
            speed = jnp.where(came, arrived(3 + c, x), half[c, x])
            vel[c, x] = jnp.where(live, speed, 0.0)
    for side in range(2):
        for c in range(3):
            zsend[side, c, SX:8] = jnp.full((8 - SX, CAP), FAR, F32)

    copies = []

    def send(src, dst, ssem, rsem, step):
        copy = pltpu.make_async_remote_copy(
            src_ref=src, dst_ref=dst, send_sem=ssem, recv_sem=rsem, device_id=at(*step), device_id_type=MESH
        )
        copy.start()
        copies.append(copy)

    for i, dy in enumerate((1, -1)):
        send(own, yblk.at[i], bsend.at[i], brecv.at[i], (0, dy, 0))
    for dy in (1, -1, 0):
        there = 1 - dy
        for s, x in ((0, 0), (1, SX - 1)):
            send(own.at[:, x], slab.at[there, s], ssend.at[there, s], srecv.at[there, s], (1, dy, 0))
    for dy in (1, -1, 0):
        there = 1 - dy
        for dx in (0, 1):
            for zi, dz in ((0, -1), (1, 1)):
                send(zsend.at[zi], zrow.at[there, dx, 1 - zi], zs.at[there, dx, zi], zr.at[there, dx, 1 - zi], (dx, dy, dz))
    for post in posts:
        post.wait_send()
    for copy in copies:
        copy.wait_send()
    for i, dy in enumerate((1, -1)):
        pltpu.make_async_remote_copy(
            src_ref=own, dst_ref=yblk.at[i], send_sem=bsend.at[i], recv_sem=brecv.at[i],
            device_id=at(0, dy, 0), device_id_type=MESH).wait_recv()
    for y in range(3):
        for s in range(2):
            pltpu.make_async_remote_copy(
                src_ref=own.at[:, 0], dst_ref=slab.at[y, s], send_sem=ssend.at[y, s], recv_sem=srecv.at[y, s],
                device_id=at(1, 0, 0), device_id_type=MESH).wait_recv()
        for g in range(2):
            for s in range(2):
                pltpu.make_async_remote_copy(
                    src_ref=zsend.at[0], dst_ref=zrow.at[y, g, s], send_sem=zs.at[y, g, s], recv_sem=zr.at[y, g, s],
                    device_id=at(0, 0, 1), device_id_type=MESH).wait_recv()


def force_kernel(own, vel, yblk, slab, zrow, out_places, out_velocity, out_forces,
                 near, packed, lists, columns, force_columns, totals):
    sub8 = iota((8, CAP), 0)
    lane8 = iota((8, CAP), 1)

    for y in range(3):
        for c in range(3):
            for xi in range(8):
                if xi == 0:
                    tile = slab[y, 1, c]
                    low, high = (zrow[y, 1, s, c, SX - 1 : SX] for s in (0, 1))
                elif xi == 7:
                    tile = slab[y, 0, c]
                    low, high = (zrow[y, 1, s, c, 0:1] for s in (0, 1))
                else:
                    tile = own[c, xi - 1] if y == 1 else yblk[y // 2, c, xi - 1]
                    low, high = (zrow[y, 0, s, c, xi - 1 : xi] for s in (0, 1))
                below = jnp.where(sub8 == 0, jnp.broadcast_to(low, (8, CAP)), pltpu.roll(tile, 1, 0))
                above = jnp.where(sub8 == SZ - 1, jnp.broadcast_to(high, (8, CAP)), pltpu.roll(tile, 7, 0))
                for zi, value in enumerate((below, tile, above)):
                    if c == 1 and y != 1:
                        value = value + (y - 1) * SIDE[1]
                    if c == 2 and zi != 1:
                        value = value + (zi - 1) * SIDE[2]
                    near[zi, c, y, xi] = value

    prefix = (iota((CAP, CAP), 0) <= iota((CAP, CAP), 1)).astype(jnp.bfloat16)
    weights = jnp.concatenate([prefix, jnp.ones((CAP, CAP), jnp.bfloat16)], axis=1)
    lane6 = iota((SZ, CAP), 1)
    steps = [(0, 0, 0)] + [
        (dx, dy, dz) for dx in (-1, 0, 1) for dy in (-1, 0, 1) for dz in (-1, 0, 1) if (dx, dy, dz) != (0, 0, 0)
    ]

    def one_row(x, _):
        mine = [near[1, c, 1, x + 1] for c in range(3)]
        live = mine[0] < 0.5 * FAR
        low = [
            jnp.broadcast_to(jnp.min(mine[c], axis=1, keepdims=True) - REACH, (8, CAP)) for c in range(3)
        ]
        high = [
            jnp.broadcast_to(
                jnp.max(jnp.where(live, mine[c], -FAR), axis=1, keepdims=True) + REACH, (8, CAP)
            )
            for c in range(3)
        ]

        def neighbour(step):
            dx, dy, dz = step
            value = [near[dz + 1, c, dy + 1, x + 1 + dx] for c in range(3)]
            if dx:
                value[0] = value[0] + dx * SIDE[0]
            return value

        masks = []
        for step in steps:
            value = neighbour(step)
            tests = [value[c] <= high[c] if s > 0 else value[c] >= low[c] for c, s in enumerate(step) if s]
            if not any(s > 0 for s in step):
                tests.append(value[0] < 0.5 * FAR)
            hit = functools.reduce(jnp.logical_and, tests)
            masks.append(jnp.where(hit, 1.0, 0.0).astype(F32))
        ranks = jnp.dot(
            jnp.concatenate(masks, axis=0).astype(jnp.bfloat16), weights, preferred_element_type=F32
        )
        base = jnp.zeros((8, CAP), F32)
        for d, step in enumerate(steps):
            upto = ranks[8 * d : 8 * d + 8, :CAP]
            count = ranks[8 * d : 8 * d + 8, CAP:]
            base_int = base.astype(I32)
            want_int = (lane8 - base_int) & 127
            want = want_int.astype(F32)
            window = jnp.where(want < count, lax.shift_right_logical(base_int + want_int, 7), -1)
            at = jnp.zeros((8, CAP), I32)
            for width in (64, 32, 16, 8, 4, 2, 1):
                seen = jnp.take_along_axis(upto, at + (width - 1), axis=1)
                at = jnp.where(seen <= want, at + width, at)
            value = neighbour(step)
            packed[d, 3] = window.astype(F32)
            for c in range(3):
                packed[d, c] = jnp.take_along_axis(value[c], at & 127, axis=1)
            base = base + count
        total = base.astype(I32)
        used = jnp.max(jnp.where(live, lane8 + 1, 0).astype(F32), axis=1, keepdims=True).astype(I32)
        list_steps = lax.shift_right_logical(total + (128 * NL - 1), 7 + (NL - 1))
        row_steps = lax.shift_right_logical(jnp.broadcast_to(used, (8, CAP)) + (8 * ROWS - 1), 3 + {1: 0, 2: 1, 4: 2, 8: 3}[ROWS])
        totals[0] = list_steps
        totals[1] = row_steps
        longest = jnp.max(list_steps)

        def fill(t, _):
            tf = t.astype(F32)
            got = [jnp.full((8, CAP), FAR, F32)] * 3
            for d in range(NDIR):
                hit = packed[d, 3] == tf
                got = [jnp.where(hit, packed[d, c], got[c]) for c in range(3)]
            for c in range(3):
                lists[t, c] = got[c]
            return 0

        lax.fori_loop(0, longest * NL, fill, 0)

        columns[...] = jnp.concatenate(mine + [jnp.zeros((CAP - 24, CAP), F32)], axis=0).T
        force_columns[...] = jnp.zeros((CAP, CAP), F32)

        for z in range(SZ):
            n_list = totals[0, z, 0]
            n_rows = totals[1, z, 0]

            def row_group(g, _):
                start = pl.multiple_of(g * (8 * ROWS), 8 * ROWS)
                block = columns[pl.ds(start, 8 * ROWS), :]
                rows = [
                    [
                        jnp.broadcast_to(block[8 * i : 8 * i + 8, 8 * c + z : 8 * c + z + 1], (8, CAP))
                        for c in range(3)
                    ]
                    for i in range(ROWS)
                ]

                def list_step(t, sums):
                    sums = list(sums)
                    for u in range(NL):
                        other = [
                            jnp.broadcast_to(lists[t * NL + u, c, z : z + 1, :], (8, CAP)) for c in range(3)
                        ]
                        for i in range(ROWS):
                            delta = [rows[i][c] - other[c] for c in range(3)]
                            square = delta[0] * delta[0] + delta[1] * delta[1] + delta[2] * delta[2]
                            inside = (square < RC * RC) & (square > 0.0)
                            root = lax.rsqrt(jnp.where(inside, square, 1.0))
                            inverse = root * root
                            sixth = inverse * inverse * inverse
                            size = inverse * sixth * (48.0 * sixth - 24.0) - EDGE * root
                            size = jnp.where(inside, size, 0.0)
                            for c in range(3):
                                sums[3 * i + c] = sums[3 * i + c] + delta[c] * size
                    return tuple(sums)

                sums = lax.fori_loop(
                    0, n_list, list_step, tuple(jnp.zeros((8, CAP), F32) for _ in range(3 * ROWS))
                )
                for c in range(3):
                    column = jnp.concatenate(
                        [jnp.sum(sums[3 * i + c], axis=1, keepdims=True) for i in range(ROWS)], axis=0
                    )
                    force_columns[pl.ds(start, 8 * ROWS), 8 * c + z : 8 * c + z + 1] = column
                return 0

            lax.fori_loop(0, n_rows, row_group, 0)

        forces = force_columns[...].T
        for c in range(3):
            live6 = live[:SZ]
            force = jnp.where(live6, forces[8 * c : 8 * c + SZ], 0.0)
            out_forces[c, x] = force
            out_velocity[c, x] = vel[c, x] + 0.5 * STEP * force
            out_places[c, x] = jnp.where(live6, mine[c][:SZ], 0.0)
        return 0

    lax.fori_loop(0, SX, one_row, 0)


def per_device(sizes, places, velocity, forces_old, counts, mig_atom, mig_face):
    shape = places.shape
    flat = (3, SX, SZ, CAP)
    vmem = pl.BlockSpec(memory_space=pltpu.VMEM)
    smem = pl.BlockSpec(memory_space=pltpu.SMEM)
    dma = pltpu.SemaphoreType.DMA
    halo = pl.pallas_call(
        functools.partial(exchange_kernel, sizes),
        out_shape=[
            jax.ShapeDtypeStruct((3, SX, 8, CAP), F32),
            jax.ShapeDtypeStruct(flat, F32),
            jax.ShapeDtypeStruct((2, 3, SX, 8, CAP), F32),
            jax.ShapeDtypeStruct((3, 2, 3, 8, CAP), F32),
            jax.ShapeDtypeStruct((3, 2, 2, 3, 8, CAP), F32),
        ],
        in_specs=[smem] * 3 + [vmem] * 3,
        out_specs=[vmem] * 5,
        scratch_shapes=[
            pltpu.VMEM(flat, F32),
            pltpu.VMEM(flat, F32),
            pltpu.VMEM((8, CAP), F32),
            pltpu.VMEM((5, 8, CAP), F32),
            pltpu.VMEM((2, 3, 8, CAP), F32),
            dma((5,)), dma((5,)), dma((2,)), dma((2,)), dma((3, 2)), dma((3, 2)), dma((3, 2, 2)), dma((3, 2, 2)),
        ],
        compiler_params=pltpu.CompilerParams(collective_id=0, has_side_effects=True),
        name="exchange",
    )(counts, mig_atom, mig_face, places.reshape(flat), velocity.reshape(flat), forces_old.reshape(flat))
    outs = pl.pallas_call(
        force_kernel,
        out_shape=[jax.ShapeDtypeStruct(flat, F32)] * 3,
        in_specs=[vmem] * 5,
        out_specs=[vmem] * 3,
        scratch_shapes=[
            pltpu.VMEM((3, 3, 3, 8, 8, CAP), F32),
            pltpu.VMEM((NDIR, 4, 8, CAP), F32),
            pltpu.VMEM((NT, 3, 8, CAP), F32),
            pltpu.VMEM((CAP, CAP), F32),
            pltpu.VMEM((CAP, CAP), F32),
            pltpu.VMEM((2, 8, CAP), I32),
        ],
        name="forces",
    )(*halo)
    return tuple(out.reshape(shape) for out in outs)


def solution(mesh):
    sizes = tuple(mesh.shape[a] for a in ("gx", "gy", "gz"))
    block = P(None, "gx", "gy", "gz", None)
    moves = P("gx", "gy", "gz", None)
    return jax.shard_map(
        functools.partial(per_device, sizes),
        mesh=mesh,
        in_specs=(block, block, block, P("gx", "gy", "gz"), moves, moves),
        out_specs=(block, block, block),
        check_vma=False,
    )
```

time: 200 us -> 60.9 us (0.30)
  the two profiles are of different devices: /device:TPU:1 before, /device:TPU:32 now
where the time goes in v1:
time: 60.9 us; the launch traced here: 59.7 us
  Pallas kernels  53.8 us (88%)
  local copies, waits for them, and re-layouts  5.32 us (9%)
  between operations  0.66 us (1%)
    pallas_call x1, Pallas kernels, per_device(): pl.pallas_call(force_kernel, out_shape=[jax.ShapeDtypeStruct(flat, F32)]...  32.8 us
    pallas_call x1, Pallas kernels, per_device(): pl.pallas_call(functools.partial(exchange_kernel, sizes), out_shape=[jax....  21 us
    unnamed x13, local copies, waits for them, and re-layouts  5.32 us

profile of v1, /device:TPU:32, one launch (start us, length us, event | category | flops | bytes accessed | tf_op | source)
XLA Modules:
  0.0 59.7 jit_solution(14661593280864950261)
XLA Ops:
  0.6 0.0 copy-start.2
  0.6 0.0 copy-start.3
  0.7 1.5 %copy.18 = f32[3,6,1,6,128]{4,3,2,1,0:T(8,128)} copy(f32[3,6,1,6,128]{4,2,3,1,0:T(1,128)} %param.6) | data formatting | bytes 110592
  2.1 0.0 copy-done.2
  2.1 0.0 copy-done.3
  2.1 0.7 %copy_bitcast_fusion = (f32[3,6,6,128]{3,2,1,0:T(8,128)}, f32[3,6,6,128]{3,2,1,0:T(8,128)}) fusion(f32[3,6,1,6,128]{4,2,3,1,0:T(1,128)S(1)} %copy-done.2, f32[3,6,1,6,128]{4,2,3,1,0:T(1,128)S(1)} %copy-done.3), kind=kLoop, calls=%fused_computation | loop fusion | bytes 221184
  2.8 21.0 %exchange.1 = (f32[3,6,8,128]{3,2,1,0:T(8,128)}, f32[3,6,6,128]{3,2,1,0:T(8,128)}, f32[2,3,6,8,128]{4,3,2,1,0:T(8,128)}, f32[3,2,3,8,128]{4,3,2,1,0:T(8,128)}, f32[3,2,2,3,8,128]{5,4,3,2,1,0:T(8,128)}) custom-call(s32[6,1,6]{2,1,0:T(1,128)} %counts.1, s32[1,1,1,16]{3,2,1,0:T(1,128)} %atoms.1, s32[1,1,1,16]{3,2,1,0:T(1,128)} %faces.1, ...), custom_call_target="tpu_custom_call" | custom-call | tf_op jit(solution)/shard_map/exchange/pallas_call | solution.py:373
  23.8 32.8 %forces.1 = (f32[3,6,6,128]{3,2,1,0:T(8,128)}, f32[3,6,6,128]{3,2,1,0:T(8,128)}, f32[3,6,6,128]{3,2,1,0:T(8,128)}) custom-call(f32[3,6,8,128]{3,2,1,0:T(8,128)} %get-tuple-element.11.own, f32[3,6,6,128]{3,2,1,0:T(8,128)} %get-tuple-element.12.vel, f32[2,3,6,8,128]{4,3,2,1,0:T(8,128)} %get-tuple-element.13.yblk, f32[3,2,3,8,128]{4,3,2,1,0:T(8,128)} %get-tuple-element.14.slab, ...), custom_call_target="tpu_custom_call" | custom-call | tf_op jit(solution)/shard_map/forces/pallas_call | solution.py:395
  56.6 0.0 copy-start.1
  56.6 1.6 %copy.9 = f32[3,6,1,6,128]{4,2,3,1,0:T(1,128)} copy(f32[3,6,1,6,128]{4,3,1,0,2:T(8,128)} %bitcast.13) | data formatting | bytes 110592
  58.2 0.0 copy-start
  58.2 0.0 copy-done.1
  58.2 0.7 %copy.10 = f32[3,6,1,6,128]{4,2,3,1,0:T(1,128)} copy(f32[3,6,1,6,128]{4,3,1,0,2:T(8,128)S(1)} %bitcast.12) | data formatting | bytes 110592
  58.9 0.2 copy-done
  59.1 0.7 %copy.11 = f32[3,6,1,6,128]{4,2,3,1,0:T(1,128)} copy(f32[3,6,1,6,128]{4,3,1,0,2:T(8,128)S(1)} %bitcast.11) | data formatting | bytes 110592
Async XLA Ops:
  0.6 1.5 %copy-start.2 = (f32[3,6,1,6,128]{4,2,3,1,0:T(1,128)S(1)}, f32[3,6,1,6,128]{4,2,3,1,0:T(1,128)}, u32[]{:S(2)}) copy-start(f32[3,6,1,6,128]{4,2,3,1,0:T(1,128)} %param.8) | copy-start | bytes 165892
  0.6 1.5 %copy-start.3 = (f32[3,6,1,6,128]{4,2,3,1,0:T(1,128)S(1)}, f32[3,6,1,6,128]{4,2,3,1,0:T(1,128)}, u32[]{:S(2)}) copy-start(f32[3,6,1,6,128]{4,2,3,1,0:T(1,128)} %param.7) | copy-start | bytes 165892
  56.6 1.6 %copy-start.1 = (f32[3,6,6,128]{3,2,1,0:T(8,128)S(1)}, f32[3,6,6,128]{3,2,1,0:T(8,128)}, u32[]{:S(2)}) copy-start(f32[3,6,6,128]{3,2,1,0:T(8,128)} %get-tuple-element.17) | copy-start | bytes 165892
  58.2 0.9 %copy-start = (f32[3,6,6,128]{3,2,1,0:T(8,128)S(1)}, f32[3,6,6,128]{3,2,1,0:T(8,128)}, u32[]{:S(2)}) copy-start(f32[3,6,6,128]{3,2,1,0:T(8,128)} %get-tuple-element.18) | copy-start | bytes 165892

commit v2 on v1

--- a/solution.py
+++ b/solution.py
@@ -22,6 +22,7 @@
 ROWS = 4
 NL = 2
 NT = 32
+GROUP = 8 * ROWS
 
 
 def iota(shape, dim):
@@ -203,7 +204,7 @@
 
 
 def force_kernel(own, vel, yblk, slab, zrow, out_places, out_velocity, out_forces,
-                 near, packed, lists, columns, force_columns, totals):
+                 near, packed, lists, columns, force_columns, splat, sums_of, totals):
     sub8 = iota((8, CAP), 0)
     lane8 = iota((8, CAP), 1)
 
@@ -239,11 +240,11 @@
         mine = [near[1, c, 1, x + 1] for c in range(3)]
         live = mine[0] < 0.5 * FAR
         low = [
-            jnp.broadcast_to(jnp.min(mine[c], axis=1, keepdims=True) - REACH, (8, CAP)) for c in range(3)
+            jnp.broadcast_to(jnp.min(mine[c], axis=1, keepdims=True), (8, CAP)) for c in range(3)
         ]
         high = [
             jnp.broadcast_to(
-                jnp.max(jnp.where(live, mine[c], -FAR), axis=1, keepdims=True) + REACH, (8, CAP)
+                jnp.max(jnp.where(live, mine[c], -FAR), axis=1, keepdims=True), (8, CAP)
             )
             for c in range(3)
         ]
@@ -258,10 +259,15 @@
         masks = []
         for step in steps:
             value = neighbour(step)
-            tests = [value[c] <= high[c] if s > 0 else value[c] >= low[c] for c, s in enumerate(step) if s]
+            gaps = [value[c] - high[c] if s > 0 else low[c] - value[c] for c, s in enumerate(step) if s]
+            if len(gaps) > 1:
+                gaps = [jnp.maximum(gap, 0.0) for gap in gaps]
+                hit = sum(gap * gap for gap in gaps) < REACH * REACH
+            elif gaps:
+                hit = gaps[0] < REACH
             if not any(s > 0 for s in step):
-                tests.append(value[0] < 0.5 * FAR)
-            hit = functools.reduce(jnp.logical_and, tests)
+                alive = value[0] < 0.5 * FAR
+                hit = hit & alive if gaps else alive
             masks.append(jnp.where(hit, 1.0, 0.0).astype(F32))
         ranks = jnp.dot(
             jnp.concatenate(masks, axis=0).astype(jnp.bfloat16), weights, preferred_element_type=F32
@@ -304,22 +310,26 @@
         lax.fori_loop(0, longest * NL, fill, 0)
 
         columns[...] = jnp.concatenate(mine + [jnp.zeros((CAP - 24, CAP), F32)], axis=0).T
-        force_columns[...] = jnp.zeros((CAP, CAP), F32)
+        most_groups = jnp.max(row_steps)
+
+        def spread(g, _):
+            start = pl.multiple_of(g * GROUP, GROUP)
+            block = columns[pl.ds(start, GROUP), :]
+            for z in range(SZ):
+                for c in range(3):
+                    splat[3 * z + c, pl.ds(start, GROUP), :] = jnp.broadcast_to(
+                        block[:, 8 * c + z : 8 * c + z + 1], (GROUP, CAP)
+                    )
+            return 0
+
+        lax.fori_loop(0, most_groups, spread, 0)
 
         for z in range(SZ):
             n_list = totals[0, z, 0]
             n_rows = totals[1, z, 0]
 
             def row_group(g, _):
-                start = pl.multiple_of(g * (8 * ROWS), 8 * ROWS)
-                block = columns[pl.ds(start, 8 * ROWS), :]
-                rows = [
-                    [
-                        jnp.broadcast_to(block[8 * i : 8 * i + 8, 8 * c + z : 8 * c + z + 1], (8, CAP))
-                        for c in range(3)
-                    ]
-                    for i in range(ROWS)
-                ]
+                start = pl.multiple_of(g * GROUP, GROUP)
 
                 def list_step(t, sums):
                     sums = list(sums)
@@ -328,14 +338,14 @@
                             jnp.broadcast_to(lists[t * NL + u, c, z : z + 1, :], (8, CAP)) for c in range(3)
                         ]
                         for i in range(ROWS):
-                            delta = [rows[i][c] - other[c] for c in range(3)]
+                            rows = pl.ds(pl.multiple_of(start + 8 * i, 8), 8)
+                            delta = [splat[3 * z + c, rows, :] - other[c] for c in range(3)]
                             square = delta[0] * delta[0] + delta[1] * delta[1] + delta[2] * delta[2]
-                            inside = (square < RC * RC) & (square > 0.0)
-                            root = lax.rsqrt(jnp.where(inside, square, 1.0))
-                            inverse = root * root
-                            sixth = inverse * inverse * inverse
-                            size = inverse * sixth * (48.0 * sixth - 24.0) - EDGE * root
-                            size = jnp.where(inside, size, 0.0)
+                            root = lax.rsqrt(jnp.maximum(square, 0.01))
+                            second = root * root
+                            sixth = second * second * second
+                            size = root * ((root * sixth) * (sixth - 0.5) - EDGE / 48.0)
+                            size = jnp.where(square < RC * RC, size, 0.0)
                             for c in range(3):
                                 sums[3 * i + c] = sums[3 * i + c] + delta[c] * size
                     return tuple(sums)
@@ -343,19 +353,32 @@
                 sums = lax.fori_loop(
                     0, n_list, list_step, tuple(jnp.zeros((8, CAP), F32) for _ in range(3 * ROWS))
                 )
-                for c in range(3):
-                    column = jnp.concatenate(
-                        [jnp.sum(sums[3 * i + c], axis=1, keepdims=True) for i in range(ROWS)], axis=0
-                    )
-                    force_columns[pl.ds(start, 8 * ROWS), 8 * c + z : 8 * c + z + 1] = column
+                for i in range(ROWS):
+                    for c in range(3):
+                        rows = pl.ds(pl.multiple_of(start + 8 * i, 8), 8)
+                        sums_of[3 * z + c, rows, :] = sums[3 * i + c]
                 return 0
 
             lax.fori_loop(0, n_rows, row_group, 0)
+
+        def gather_sums(g, _):
+            start = pl.multiple_of(g * GROUP, GROUP)
+            for i in range(ROWS):
+                rows = pl.ds(pl.multiple_of(start + 8 * i, 8), 8)
+                block = jnp.zeros((8, CAP), F32)
+                for z in range(SZ):
+                    for c in range(3):
+                        total = jnp.sum(sums_of[3 * z + c, rows, :], axis=1, keepdims=True)
+                        block = jnp.where(lane8 == 8 * c + z, total, block)
+                force_columns[rows, :] = block
+            return 0
+
+        lax.fori_loop(0, most_groups, gather_sums, 0)
 
         forces = force_columns[...].T
         for c in range(3):
             live6 = live[:SZ]
-            force = jnp.where(live6, forces[8 * c : 8 * c + SZ], 0.0)
+            force = jnp.where(live6, 48.0 * forces[8 * c : 8 * c + SZ], 0.0)
             out_forces[c, x] = force
             out_velocity[c, x] = vel[c, x] + 0.5 * STEP * force
             out_places[c, x] = jnp.where(live6, mine[c][:SZ], 0.0)
@@ -403,6 +426,8 @@
             pltpu.VMEM((NT, 3, 8, CAP), F32),
             pltpu.VMEM((CAP, CAP), F32),
             pltpu.VMEM((CAP, CAP), F32),
+            pltpu.VMEM((3 * SZ, CAP, CAP), F32),
+            pltpu.VMEM((3 * SZ, CAP, CAP), F32),
             pltpu.VMEM((2, 8, CAP), I32),
         ],
         name="forces",

time: 60.9 us -> 48.5 us (0.80)
  the two profiles are of different devices: /device:TPU:32 before, /device:TPU:1 now
where the time goes in v2:
time: 48.5 us; the launch traced here: 47.6 us
  Pallas kernels  41.7 us (86%)
  local copies, waits for them, and re-layouts  5.32 us (11%)
  between operations  0.66 us (1%)
    pallas_call x1, Pallas kernels, per_device(): pl.pallas_call(functools.partial(exchange_kernel, sizes), out_shape=[jax....  22.5 us
    pallas_call x1, Pallas kernels, per_device(): pl.pallas_call(force_kernel, out_shape=[jax.ShapeDtypeStruct(flat, F32)]...  19.1 us
    unnamed x13, local copies, waits for them, and re-layouts  5.32 us

profile of v2, /device:TPU:1, one launch (start us, length us, event | category | flops | bytes accessed | tf_op | source)
XLA Modules:
  0.0 47.6 jit_solution(10763794635057618878)
XLA Ops:
  0.6 0.0 copy-start.2
  0.6 0.0 copy-start.3
  0.7 1.5 %copy.18 = f32[3,6,1,6,128]{4,3,2,1,0:T(8,128)} copy(f32[3,6,1,6,128]{4,2,3,1,0:T(1,128)} %param.6) | data formatting | bytes 110592
  2.1 0.0 copy-done.2
  2.1 0.0 copy-done.3
  2.1 0.7 %copy_bitcast_fusion = (f32[3,6,6,128]{3,2,1,0:T(8,128)}, f32[3,6,6,128]{3,2,1,0:T(8,128)}) fusion(f32[3,6,1,6,128]{4,2,3,1,0:T(1,128)S(1)} %copy-done.2, f32[3,6,1,6,128]{4,2,3,1,0:T(1,128)S(1)} %copy-done.3), kind=kLoop, calls=%fused_computation | loop fusion | bytes 221184
  2.8 22.5 %exchange.1 = (f32[3,6,8,128]{3,2,1,0:T(8,128)}, f32[3,6,6,128]{3,2,1,0:T(8,128)}, f32[2,3,6,8,128]{4,3,2,1,0:T(8,128)}, f32[3,2,3,8,128]{4,3,2,1,0:T(8,128)}, f32[3,2,2,3,8,128]{5,4,3,2,1,0:T(8,128)}) custom-call(s32[6,1,6]{2,1,0:T(1,128)} %counts.1, s32[1,1,1,16]{3,2,1,0:T(1,128)} %atoms.1, s32[1,1,1,16]{3,2,1,0:T(1,128)} %faces.1, ...), custom_call_target="tpu_custom_call" | custom-call | tf_op jit(solution)/shard_map/exchange/pallas_call | solution.py:396
  25.3 19.1 %forces.1 = (f32[3,6,6,128]{3,2,1,0:T(8,128)}, f32[3,6,6,128]{3,2,1,0:T(8,128)}, f32[3,6,6,128]{3,2,1,0:T(8,128)}) custom-call(f32[3,6,8,128]{3,2,1,0:T(8,128)} %get-tuple-element.11.own, f32[3,6,6,128]{3,2,1,0:T(8,128)} %get-tuple-element.12.vel, f32[2,3,6,8,128]{4,3,2,1,0:T(8,128)} %get-tuple-element.13.yblk, f32[3,2,3,8,128]{4,3,2,1,0:T(8,128)} %get-tuple-element.14.slab, ...), custom_call_target="tpu_custom_call" | custom-call | tf_op jit(solution)/shard_map/forces/pallas_call | solution.py:418
  44.5 0.0 copy-start.1
  44.5 1.6 %copy.9 = f32[3,6,1,6,128]{4,2,3,1,0:T(1,128)} copy(f32[3,6,1,6,128]{4,3,1,0,2:T(8,128)} %bitcast.13) | data formatting | bytes 110592
  46.1 0.0 copy-start
  46.1 0.0 copy-done.1
  46.1 0.7 %copy.10 = f32[3,6,1,6,128]{4,2,3,1,0:T(1,128)} copy(f32[3,6,1,6,128]{4,3,1,0,2:T(8,128)S(1)} %bitcast.12) | data formatting | bytes 110592
  46.7 0.2 copy-done
  46.9 0.7 %copy.11 = f32[3,6,1,6,128]{4,2,3,1,0:T(1,128)} copy(f32[3,6,1,6,128]{4,3,1,0,2:T(8,128)S(1)} %bitcast.11) | data formatting | bytes 110592
Async XLA Ops:
  0.6 1.5 %copy-start.2 = (f32[3,6,1,6,128]{4,2,3,1,0:T(1,128)S(1)}, f32[3,6,1,6,128]{4,2,3,1,0:T(1,128)}, u32[]{:S(2)}) copy-start(f32[3,6,1,6,128]{4,2,3,1,0:T(1,128)} %param.8) | copy-start | bytes 165892
  0.6 1.5 %copy-start.3 = (f32[3,6,1,6,128]{4,2,3,1,0:T(1,128)S(1)}, f32[3,6,1,6,128]{4,2,3,1,0:T(1,128)}, u32[]{:S(2)}) copy-start(f32[3,6,1,6,128]{4,2,3,1,0:T(1,128)} %param.7) | copy-start | bytes 165892
  44.5 1.6 %copy-start.1 = (f32[3,6,6,128]{3,2,1,0:T(8,128)S(1)}, f32[3,6,6,128]{3,2,1,0:T(8,128)}, u32[]{:S(2)}) copy-start(f32[3,6,6,128]{3,2,1,0:T(8,128)} %get-tuple-element.17) | copy-start | bytes 165892
  46.1 0.9 %copy-start = (f32[3,6,6,128]{3,2,1,0:T(8,128)S(1)}, f32[3,6,6,128]{3,2,1,0:T(8,128)}, u32[]{:S(2)}) copy-start(f32[3,6,6,128]{3,2,1,0:T(8,128)} %get-tuple-element.18) | copy-start | bytes 165892
